TPU v7x, 32 devices: a whole 2x2x4 slice. The times are simulated.
32 devices in a mesh: dp: 16 (over z, y, x), rep: 2 (over core).
Axes of the slice: x: 2, y: 2, z: 4, core: 2. Of those that a mesh axis runs over, the one named last changes fastest.
Arguments:
- table: float32 [131072, 400], P(('dp', 'rep')), may hold values from -6 to 6
- batch_index: int32 [32768], P(('dp', 'rep')), may hold values from 0 to 4095
- labels: int32 [32768], P(('dp', 'rep')), may hold values from 0 to 46
- w_branch: float32 [4, 100, 512], P(None, None, 'dp'), may hold values from -0.625 to 0.625
- w_merge: float32 [2048, 512], P('dp'), may hold values from -0.125 to 0.125
- w_class: float32 [512, 47], P('dp'), may hold values from -0.5 to 0.5
- small_params: float32 [20, 512], P(None, 'dp'), as said below
- first_branch: float32 [4, 100, 512], P(None, None, 'dp'), may hold values from -0.0014648438 to 0.0014648438
- first_merge: float32 [2048, 512], P('dp'), may hold values from -0.0014648438 to 0.0014648438
- first_class: float32 [512, 47], P('dp'), may hold values from -0.0014648438 to 0.0014648438
- first_small: float32 [20, 512], P(None, 'dp'), may hold values from -0.00390625 to 0.00390625
- second_branch: float32 [4, 100, 512], P(None, None, 'dp'), may hold values from 7.7659046e-10 to 3.1063618e-09
- second_merge: float32 [2048, 512], P('dp'), may hold values from 7.7659046e-10 to 3.1063618e-09
- second_class: float32 [512, 47], P('dp'), may hold values from 7.7659046e-10 to 3.1063618e-09
- second_small: float32 [20, 512], P(None, 'dp'), may hold values from 6.989314e-09 to 2.7957256e-08
Outputs:
- new_branch: float32 [4, 100, 512], P(None, None, 'dp')
- new_merge: float32 [2048, 512], P('dp')
- new_class: float32 [512, 47], P('dp')
- new_small: float32 [20, 512], P(None, 'dp')
- moment_branch: float32 [4, 100, 512], P(None, None, 'dp')
- moment_merge: float32 [2048, 512], P('dp')
- moment_class: float32 [512, 47], P('dp')
- moment_small: float32 [20, 512], P(None, 'dp')
- square_branch: float32 [4, 100, 512], P(None, None, 'dp')
- square_merge: float32 [2048, 512], P('dp')
- square_class: float32 [512, 47], P('dp')
- square_small: float32 [20, 512], P(None, 'dp')
- copy_branch: bfloat16 [4, 100, 512], P(None, None, 'dp')
- copy_merge: bfloat16 [2048, 512], P('dp')
- copy_class: bfloat16 [512, 47], P('dp')
- copy_small: bfloat16 [20, 512], P(None, 'dp')
- grad_norm: float32 [], replicated
- row_grads: float32 [32768, 400], P(('dp', 'rep'))
Inputs may be any that keep to these rules, and one draw needn't show every extreme that they name: `batch_index`: each entry indexes a row of the block of 4096 table rows that lies on the same device as the entry. `small_params`: gains lie in 0.3 to 2.0, slopes in 0.05 to 0.45.
All inputs are finite; a program needn't handle non-finite values.
Results may differ from a plain program's by a relative error of at most 0.011.
Values may be sent and summed in bfloat16 or wider, within the bound.
No kernel may reach another device: no remote copies, remote signals or barrier semaphores. Data moves between devices by JAX's collectives and lax.ppermute only.
A program may use at most 128 MiB of HBM per device.

v0:
```python
import jax
import jax.numpy as jnp
from jax import lax
from jax.sharding import PartitionSpec as P

HOPS = 4
STEP = 7
EPS_NORM = 1e-05


def leaky(value, slope):
    return slope * value + (1.0 - slope) * value * jax.nn.sigmoid(value)


def leaky_back(upstream, value, slope):
    sig = jax.nn.sigmoid(value)
    slope_term = jnp.sum(upstream * value * (1.0 - sig), axis=0)
    derivative = slope + (1.0 - slope) * (sig + value * sig * (1.0 - sig))
    return (upstream * derivative, slope_term)


def cross_dot(left, right):
    return lax.dot_general(
        left, right, (((0,), (0,)), ((), ())), preferred_element_type=jnp.float32
    )


def back_dot(left, right):
    return lax.dot_general(
        left, right, (((1,), (1,)), ((), ())), preferred_element_type=jnp.float32
    )


def adamw(weight, grad, moment, square, scale, rate):
    clipped = grad * scale
    moment_new = 0.9 * moment + 0.1 * clipped
    square_new = 0.999 * square + 0.001 * clipped * clipped
    fix_one = 1.0 - 0.9**STEP
    fix_two = 1.0 - 0.999**STEP
    update = moment_new / fix_one / (jnp.sqrt(square_new / fix_two) + 1e-08) + 0.01 * weight
    weight_new = weight - rate * update
    return (weight_new, moment_new, square_new)


def on_device(
    table,
    batch_index,
    labels,
    w_branch,
    w_merge,
    w_class,
    small_params,
    first_branch,
    first_merge,
    first_class,
    first_small,
    second_branch,
    second_merge,
    second_class,
    second_small,
):
    batch = batch_index.shape[0]
    row_count = batch * lax.axis_size("dp") * lax.axis_size("rep")
    d_in = w_branch.shape[1]
    hidden = w_merge.shape[1]
    hidden_width = HOPS * hidden
    classes = w_class.shape[1]
    rows = jnp.take(table, batch_index, axis=0)
    input_features = rows.astype(jnp.bfloat16).reshape(batch, HOPS, d_in)
    branch_full, merge_full, class_full, small_full = (
        lax.all_gather(w_branch.astype(jnp.bfloat16), "dp", axis=2, tiled=True),
        lax.all_gather(w_merge.astype(jnp.bfloat16), "dp", axis=0, tiled=True),
        lax.all_gather(w_class.astype(jnp.bfloat16), "dp", axis=0, tiled=True),
        lax.all_gather(small_params.astype(jnp.bfloat16), "dp", axis=1, tiled=True),
    )
    params = small_full.astype(jnp.float32)
    gain1 = params[0:HOPS].reshape(hidden_width)
    shift1 = params[HOPS : 2 * HOPS].reshape(hidden_width)
    slope1 = params[2 * HOPS : 3 * HOPS].reshape(hidden_width)
    slope_join = params[3 * HOPS : 4 * HOPS].reshape(hidden_width)
    gain2 = params[4 * HOPS]
    shift2 = params[4 * HOPS + 1]
    slope2 = params[4 * HOPS + 2]
    bias3 = params[4 * HOPS + 3, :classes]
    first_pre = jnp.einsum(
        "fsq,sqv->fsv", input_features, branch_full, preferred_element_type=jnp.float32
    ).reshape(batch, hidden_width)
    sums_one = lax.psum(
        (jnp.sum(first_pre, axis=0), jnp.sum(first_pre * first_pre, axis=0)), ("dp", "rep")
    )
    mean1 = sums_one[0] / row_count
    inv1 = lax.rsqrt(sums_one[1] / row_count - mean1 * mean1 + EPS_NORM)
    norm1 = (first_pre - mean1) * inv1
    lin1 = gain1 * norm1 + shift1
    act1 = leaky(lin1, slope1)
    joined_low = leaky(act1, slope_join).astype(jnp.bfloat16)
    pre2 = jnp.dot(joined_low, merge_full, preferred_element_type=jnp.float32)
    sums_two = lax.psum((jnp.sum(pre2, axis=0), jnp.sum(pre2 * pre2, axis=0)), ("dp", "rep"))
    mean2 = sums_two[0] / row_count
    inv2 = lax.rsqrt(sums_two[1] / row_count - mean2 * mean2 + EPS_NORM)
    norm2 = (pre2 - mean2) * inv2
    lin2 = gain2 * norm2 + shift2
    act2_low = leaky(lin2, slope2).astype(jnp.bfloat16)
    logits = jnp.dot(act2_low, class_full, preferred_element_type=jnp.float32) + bias3
    probs = jax.nn.softmax(logits, axis=1)
    onehot = (labels[:, None] == jnp.arange(classes, dtype=jnp.int32)[None, :]).astype(jnp.float32)
    dlogits = (probs - onehot).astype(jnp.bfloat16)
    branch_back, merge_back, class_back = (
        lax.all_gather(w_branch.astype(jnp.bfloat16), "dp", axis=2, tiled=True),
        lax.all_gather(w_merge.astype(jnp.bfloat16), "dp", axis=0, tiled=True),
        lax.all_gather(w_class.astype(jnp.bfloat16), "dp", axis=0, tiled=True),
    )
    grad_class = cross_dot(act2_low, dlogits)
    grad_bias3 = jnp.sum(dlogits.astype(jnp.float32), axis=0)
    dact2 = back_dot(dlogits, class_back)
    dy2, grad_slope2 = leaky_back(dact2, lin2, slope2)
    gain2_part = jnp.sum(dy2 * norm2, axis=0)
    shift2_part = jnp.sum(dy2, axis=0)
    totals_two = lax.psum((shift2_part, gain2_part), ("dp", "rep"))
    dpre2 = (
        inv2
        * (
            gain2 * dy2
            - gain2 * totals_two[0] / row_count
            - norm2 * gain2 * totals_two[1] / row_count
        )
    ).astype(jnp.bfloat16)
    grad_merge = cross_dot(joined_low, dpre2)
    djoined = back_dot(dpre2, merge_back)
    dact1, grad_slope_join = leaky_back(djoined, act1, slope_join)
    dy1, grad_slope1 = leaky_back(dact1, lin1, slope1)
    gain1_part = jnp.sum(dy1 * norm1, axis=0)
    shift1_part = jnp.sum(dy1, axis=0)
    totals_one = lax.psum((shift1_part, gain1_part), ("dp", "rep"))
    first_grad = (
        inv1
        * (
            gain1 * dy1
            - gain1 * totals_one[0] / row_count
            - norm1 * gain1 * totals_one[1] / row_count
        )
    ).astype(jnp.bfloat16)
    first_grad = first_grad.reshape(batch, HOPS, hidden)
    branch_gradient = jnp.einsum(
        "pze,pzv->zev", input_features, first_grad, preferred_element_type=jnp.float32
    )
    row_grads = jnp.einsum(
        "fsz,sez->fse", first_grad, branch_back, preferred_element_type=jnp.float32
    ).reshape(batch, HOPS * d_in)
    bias_row = jnp.zeros((hidden,), jnp.float32).at[:classes].set(grad_bias3)
    grad_small = jnp.concatenate(
        [
            gain1_part.reshape(HOPS, hidden),
            shift1_part.reshape(HOPS, hidden),
            grad_slope1.reshape(HOPS, hidden),
            grad_slope_join.reshape(HOPS, hidden),
            gain2_part[None],
            shift2_part[None],
            grad_slope2[None],
            bias_row[None],
        ],
        axis=0,
    )
    paired = (
        lax.psum(branch_gradient.astype(jnp.bfloat16), "rep").astype(jnp.float32),
        lax.psum(grad_merge.astype(jnp.bfloat16), "rep").astype(jnp.float32),
        lax.psum(grad_class.astype(jnp.bfloat16), "rep").astype(jnp.float32),
        lax.psum(grad_small.astype(jnp.bfloat16), "rep").astype(jnp.float32),
    )
    shares = (
        lax.psum_scatter(paired[0], "dp", scatter_dimension=2, tiled=True),
        lax.psum_scatter(paired[1], "dp", scatter_dimension=0, tiled=True),
        lax.psum_scatter(paired[2], "dp", scatter_dimension=0, tiled=True),
        lax.psum_scatter(paired[3], "dp", scatter_dimension=1, tiled=True),
    )
    local_squares = jnp.float32(0.0)
    for share in shares:
        local_squares = local_squares + jnp.sum(share * share)
    grad_norm = jnp.sqrt(lax.psum(local_squares, "dp"))
    scale = 1.0 / jnp.maximum(grad_norm, 1.0)
    weights = (w_branch, w_merge, w_class, small_params)
    firsts = (first_branch, first_merge, first_class, first_small)
    seconds = (second_branch, second_merge, second_class, second_small)
    rates = (0.05, 0.05, 0.05, 0.3)
    results = [
        adamw(w, g, m, v, scale, r)
        for w, g, m, v, r in zip(weights, shares, firsts, seconds, rates)
    ]
    news = tuple((r[0] for r in results))
    moments = tuple((r[1] for r in results))
    squares = tuple((r[2] for r in results))
    copies = tuple((r.astype(jnp.bfloat16) for r in news))
    return (
        news[0],
        news[1],
        news[2],
        news[3],
        moments[0],
        moments[1],
        moments[2],
        moments[3],
        squares[0],
        squares[1],
        squares[2],
        squares[3],
        copies[0],
        copies[1],
        copies[2],
        copies[3],
        grad_norm,
        row_grads,
    )


def solution(mesh):
    placed = (
        P(("dp", "rep"), None),
        P(("dp", "rep")),
        P(("dp", "rep")),
        P(None, None, "dp"),
        P("dp", None),
        P("dp", None),
        P(None, "dp"),
        P(None, None, "dp"),
        P("dp", None),
        P("dp", None),
        P(None, "dp"),
        P(None, None, "dp"),
        P("dp", None),
        P("dp", None),
        P(None, "dp"),
    )
    return jax.shard_map(
        on_device,
        mesh=mesh,
        in_specs=placed,
        out_specs=(
            P(None, None, "dp"),
            P("dp", None),
            P("dp", None),
            P(None, "dp"),
            P(None, None, "dp"),
            P("dp", None),
            P("dp", None),
            P(None, "dp"),
            P(None, None, "dp"),
            P("dp", None),
            P("dp", None),
            P(None, "dp"),
            P(None, None, "dp"),
            P("dp", None),
            P("dp", None),
            P(None, "dp"),
            P(),
            P(("dp", "rep"), None),
        ),
        check_vma=False,
    )
```

profile of v0, /device:TPU:0, one launch (start us, length us, event | category | flops | bytes accessed | tf_op | source)
XLA Modules:
  0.0 804.2 jit_solution(16714491165405822003)
XLA Ops:
  7.2 1.6 convert_element_type.82
  11.8 0.8 convert_element_type.78
  12.6 43.0 %all-gather = bf16[16,32,20]{1,2,0:T(8,128)(2,1)S(1)} all-gather(bf16[1,32,20]{1,2,0:T(8,128)(2,1)S(1)} %convert_bitcast_fusion), channel_id=1, replica_groups=mesh['dp'=16,'rep'=2] {'dp'}, dimensions={0}, use_global_device_ids=true | all-gather | bytes 21760 | tf_op jit(solution)/shard_map/all_gather | solution.py:74
  55.8 40.4 %all_gather.15 = bf16[4,100,512]{1,2,0:T(8,128)(2,1)S(1)} all-gather(bf16[4,100,32]{1,2,0:T(8,128)(2,1)S(1)} %convert_element_type.78), channel_id=1, replica_groups=mesh['dp'=16,'rep'=2] {'dp'}, dimensions={2}, use_global_device_ids=true | all-gather | bytes 435200 | tf_op jit(solution)/shard_map/all_gather | solution.py:71
  96.2 6.9 copy.50
  103.1 6.7 gather_fusion
  110.5 4.5 fusion
  115.0 9.2 %copy.53 = f32[1024,2048]{1,0:T(8,128)} copy(f32[1024,2048]{0,1:T(8,128)} %bitcast.71) | data formatting | bytes 16777216 | tf_op jit(solution)/shard_map/reshape | solution.py:87
  124.2 37.0 %all-reduce.4 = (f32[2048]{0:T(1024)S(1)}, f32[2048]{0:T(1024)S(1)}) all-reduce(f32[2048]{0:T(1024)S(1)} %bitcast.97, f32[2048]{0:T(1024)S(1)} %bitcast.96), channel_id=1, replica_groups=mesh['dp'=16,'rep'=2] {'dp','rep'}, use_global_device_ids=true, to_apply=%region_3.4 | all-reduce | flops 4096 | bytes 32768 | tf_op jit(solution)/shard_map/psum | solution.py:88
  161.1 43.3 %all_gather.18 = bf16[512,47]{1,0:T(8,128)(2,1)} all-gather(bf16[32,47]{1,0:T(8,128)(2,1)S(1)} %convert_element_type.84), channel_id=1, replica_groups=mesh['dp'=16,'rep'=2] {'dp'}, dimensions={0}, use_global_device_ids=true | all-gather | bytes 51136 | tf_op jit(solution)/shard_map/all_gather | solution.py:73
  205.5 9.1 %add_convert_fusion = bf16[1024,2048]{1,0:T(8,128)(2,1)} fusion(f32[2048]{0:T(1024)S(1)} %get-tuple-element.89, f32[2048]{0:T(1024)S(1)} %bitcast.86, f32[2048]{0:T(1024)S(1)} %broadcast_subtract_fusion.1, f32[2048]{0:T(1024)S(1)} %bitcast.92, f32[2048]{0:T(1024)S(1)} %get-tuple-element.82, f32[1024,2048]{1,0:T(8,128)} %copy.53, ...), kind=kLoop, calls=%fused_computation.10 | loop fusion | flops 39845888 | bytes 12648448 | tf_op jit(solution)/shard_map/convert_element_type | solution.py:96
  214.7 5.2 multiply_reduce_fusion.5
  219.9 37.1 %all-reduce.3 = (f32[512]{0:T(512)}, f32[512]{0:T(512)}) all-reduce(f32[512]{0:T(512)S(1)} %get-tuple-element.40, f32[512]{0:T(512)S(1)} %get-tuple-element.39), channel_id=1, replica_groups=mesh['dp'=16,'rep'=2] {'dp','rep'}, use_global_device_ids=true, to_apply=%region_7.8 | all-reduce | flops 1024 | bytes 8192 | tf_op jit(solution)/shard_map/psum | solution.py:98
  257.7 1.6 add_convert_fusion.1
  259.2 1.3 fusion.32
  260.7 1.4 fusion.30
  262.0 1.1 convolution_convert_fusion.1
  263.2 4.2 multiply_reduce_fusion.3
  268.6 41.4 %all-reduce.2 = (f32[512]{0:T(512)}, f32[512]{0:T(512)}) all-reduce(f32[512]{0:T(512)} %copy-done.14, f32[512]{0:T(512)} %copy-done.15), channel_id=1, replica_groups=mesh['dp'=16,'rep'=2] {'dp','rep'}, use_global_device_ids=true, to_apply=%region_13.14 | all-reduce | flops 1024 | bytes 8192 | tf_op jit(solution)/shard_map/psum | solution.py:119
  310.0 0.8 multiply_multiply_fusion.5
  310.9 2.7 multiply_convert_fusion.1
  313.6 3.8 convolution_convert_fusion
  317.4 13.9 %multiply_reduce_fusion = (bf16[2048]{0:T(1024)(128)(2,1)S(1)}, bf16[2048]{0:T(1024)(128)(2,1)S(1)}, f32[2048]{0:T(1024)S(1)}, f32[2048]{0:T(1024)S(1)}, f32[1024,2048]{1,0:T(8,128)}) fusion(f32[2048]{0:T(1024)S(1)} %broadcast_subtract_fusion.1, f32[2048]{0:T(1024)S(1)} %bitcast.93, f32[2048]{0:T(1024)S(1)} %get-tuple-element.82, ...), kind=kOutput, calls=%fused_computation.4 | convolution fusion | flops 2225070080 | bytes 20013056 | tf_op jit(solution)/shard_map/dot_general | solution.py:29
  331.3 40.2 %all-reduce.1 = (f32[2048]{0:T(1024)S(1)}, f32[2048]{0:T(1024)S(1)}) all-reduce(f32[2048]{0:T(1024)S(1)} %get-tuple-element.32, f32[2048]{0:T(1024)S(1)} %get-tuple-element.33), channel_id=1, replica_groups=mesh['dp'=16,'rep'=2] {'dp','rep'}, use_global_device_ids=true, to_apply=%region_17.18 | all-reduce | flops 4096 | bytes 32768 | tf_op jit(solution)/shard_map/psum | solution.py:134
  371.7 1.9 concatenate.6
  373.8 7.3 multiply_convert_fusion
  381.1 1.9 copy-done
  383.0 2.5 fusion.10
  385.6 5.8 all-reduce.10.cloned.1.call-done
  391.4 1.6 copy.56
  393.1 1.6 convert_element_type.94
  394.8 23.1 %all-reduce.12.cloned.1.call-done = (bf16[4,100,512]{1,2,0:T(8,128)(2,1)}, bf16[2048,512]{1,0:T(8,128)(2,1)}) async-done(((bf16[4,100,512]{1,2,0:T(8,128)(2,1)}, bf16[2048,512]{1,0:T(8,128)(2,1)}), (bf16[4,100,512]{1,2,0:T(8,128)(2,1)}, bf16[2048,512]{1,0:T(8,128)(2,1)})) %all-reduce.12.cloned.1.call-update) | async-done | bytes 2506768 | tf_op jit(solution)/shard_map/psum | solution.py:165
  417.9 2.1 convert_element_type.90
  420.1 4.2 convert_element_type.92
  424.4 3.7 fusion.7
  428.1 69.9 %reduce-scatter.13.cloned.1.call-done = f32[32,20]{1,0:T(8,128)} async-done(((f32[512,20]{1,0:T(8,128)}), f32[32,20]{1,0:T(8,128)}) %reduce-scatter.13.cloned.1.call-update) | async-done | bytes 2576
  499.4 73.8 %reduce-scatter.11.cloned.1.call-done = f32[32,47]{1,0:T(8,128)} async-done(((f32[512,47]{1,0:T(8,128)}), f32[32,47]{1,0:T(8,128)}) %reduce-scatter.11.cloned.1.call-update) | async-done | bytes 6032 | tf_op jit(solution)/shard_map/reduce_scatter | solution.py:173
  573.1 1.3 multiply_reduce_fusion.8
  574.5 75.5 %reduce-scatter.7.cloned.1.call-done = f32[4,100,32]{1,2,0:T(8,128)} async-done(((f32[4,100,512]{1,2,0:T(8,128)}), f32[4,100,32]{1,2,0:T(8,128)}) %reduce-scatter.7.cloned.1.call-update) | async-done | bytes 51216 | tf_op jit(solution)/shard_map/reduce_scatter | solution.py:171
  650.0 1.5 multiply_reduce_fusion.7
  651.5 92.4 %reduce-scatter.9.cloned.1.call-done = f32[128,512]{1,0:T(8,128)} async-done(((f32[2048,512]{1,0:T(8,128)}), f32[128,512]{1,0:T(8,128)}) %reduce-scatter.9.cloned.1.call-update) | async-done | bytes 262160 | tf_op jit(solution)/shard_map/reduce_scatter | solution.py:172
  743.9 1.7 multiply_reduce_fusion.6
  748.2 1.3 reshape.135
  749.5 40.5 %psum.103 = f32[]{:T(128)} all-reduce(f32[]{:T(128)S(6)} %add.234), channel_id=1, replica_groups=mesh['dp'=16,'rep'=2] {'dp'}, use_global_device_ids=true, to_apply=%region_34.35 | all-reduce | flops 1 | bytes 8 | tf_op jit(solution)/shard_map/psum | solution.py:179
  790.8 1.4 fusion.22
  792.2 1.4 fusion.24
  793.5 1.6 fusion.28
  795.1 1.1 fusion.26
  (99 shorter events, 8.9 us)
Async XLA Ops:
  7.2 207.5 %all-gather.3.cloned.1.call-start = ((), (), s32[]{:S(2)}) async-start(), calls=%async_computation.4 | async-start | bytes 2228224 | tf_op jit(solution)/shard_map/all_gather | solution.py:72
  8.9 382.5 %all-reduce.10.cloned.1.call-start = ((), (), s32[]{:S(2)}) async-start(), calls=%async_computation.9 | async-start | bytes 311296 | tf_op jit(solution)/shard_map/psum | solution.py:167
  9.6 100.9 %copy-start.16 = (pred[1024]{0:T(1024)(128)(4,1)}, pred[1024]{0:T(1024)(128)(4,1)S(1)}, u32[]{:S(2)}) copy-start(pred[1024]{0:T(1024)(128)(4,1)S(1)} %compare_and_fusion) | copy-start | bytes 3076
  256.9 6.2 copy-start.4
  267.4 0.6 copy-start.14
  267.4 1.1 copy-start.15
  310.0 3.5 copy-start.1
  310.8 6.5 slice-start
  313.5 3.8 slice-start.1
  313.6 3.8 copy-start.21
  317.4 54.2 %copy-start.20 = (bf16[512]{0:T(512)(128)(2,1)S(1)}, bf16[512]{0:T(512)(128)(2,1)}, u32[]{:S(2)}) copy-start(bf16[512]{0:T(512)(128)(2,1)} %get-tuple-element.36) | copy-start | bytes 3076
  317.4 54.2 %copy-start.18 = (bf16[512]{0:T(512)(128)(2,1)S(1)}, bf16[512]{0:T(512)(128)(2,1)}, u32[]{:S(2)}) copy-start(bf16[512]{0:T(512)(128)(2,1)} %convert.38) | copy-start | bytes 3076
  317.4 54.2 %copy-start.19 = (bf16[47]{0:T(256)(128)(2,1)S(1)}, bf16[47]{0:T(256)(128)(2,1)}, u32[]{:S(2)}) copy-start(bf16[47]{0:T(256)(128)(2,1)} %get-tuple-element.69) | copy-start | bytes 286
  373.5 44.4 %all-reduce.12.cloned.1.call-start = ((), (), s32[]{:S(2)}) async-start(), calls=%async_computation.10 | async-start | bytes 5242880 | tf_op jit(solution)/shard_map/psum | solution.py:165
  373.8 9.2 %copy-start.17 = (pred[1024]{0:T(1024)(128)(4,1)S(1)}, pred[1024]{0:T(1024)(128)(4,1)}, u32[]{:S(2)}) copy-start(pred[1024]{0:T(1024)(128)(4,1)} %copy-done.16) | copy-start | bytes 3076
  381.1 1.9 copy-start
  385.5 112.5 %reduce-scatter.13.cloned.1.call-start = ((), (), s32[]{:S(2)}) async-start(), calls=%async_computation.8 | async-start | bytes 278528
  393.0 180.1 %reduce-scatter.11.cloned.1.call-start = ((), (), s32[]{:S(2)}) async-start(), calls=%async_computation.7 | async-start | bytes 278528 | tf_op jit(solution)/shard_map/reduce_scatter | solution.py:173
  394.7 255.3 %reduce-scatter.7.cloned.1.call-start = ((), (), s32[]{:S(2)}) async-start(), calls=%async_computation.5 | async-start | bytes 1114112 | tf_op jit(solution)/shard_map/reduce_scatter | solution.py:171
  420.0 323.9 %reduce-scatter.9.cloned.1.call-start = ((), (), s32[]{:S(2)}) async-start(), calls=%async_computation.6 | async-start | bytes 4456448 | tf_op jit(solution)/shard_map/reduce_scatter | solution.py:172
  424.2 366.6 %copy-start.11 = (f32[20,32]{1,0:T(8,128)S(1)}, f32[20,32]{1,0:T(8,128)}, u32[]{:S(2)}) copy-start(f32[20,32]{1,0:T(8,128)} %param.23) | copy-start | bytes 7684
  424.2 367.9 %copy-start.10 = (f32[32,47]{1,0:T(8,128)S(1)}, f32[32,47]{1,0:T(8,128)}, u32[]{:S(2)}) copy-start(f32[32,47]{1,0:T(8,128)} %param.22) | copy-start | bytes 18052
  424.3 367.9 %copy-start.12 = (f32[32,47]{1,0:T(8,128)S(1)}, f32[32,47]{1,0:T(8,128)}, u32[]{:S(2)}) copy-start(f32[32,47]{1,0:T(8,128)} %param.26) | copy-start | bytes 18052
  424.3 367.9 %copy-start.13 = (f32[32,47]{1,0:T(8,128)S(1)}, f32[32,47]{1,0:T(8,128)}, u32[]{:S(2)}) copy-start(f32[32,47]{1,0:T(8,128)} %param.30) | copy-start | bytes 18052
  424.3 369.3 %copy-start.7 = (f32[4,100,32]{1,2,0:T(8,128)S(1)}, f32[4,100,32]{1,2,0:T(8,128)}, u32[]{:S(2)}) copy-start(f32[4,100,32]{1,2,0:T(8,128)} %param.20) | copy-start | bytes 153604
  424.3 369.2 %copy-start.8 = (f32[4,100,32]{1,2,0:T(8,128)S(1)}, f32[4,100,32]{1,2,0:T(8,128)}, u32[]{:S(2)}) copy-start(f32[4,100,32]{1,2,0:T(8,128)} %param.24) | copy-start | bytes 153604
  424.3 369.2 %copy-start.9 = (f32[4,100,32]{1,2,0:T(8,128)S(1)}, f32[4,100,32]{1,2,0:T(8,128)}, u32[]{:S(2)}) copy-start(f32[4,100,32]{1,2,0:T(8,128)} %param.28) | copy-start | bytes 153604
  424.3 370.8 %copy-start.2 = (f32[128,512]{1,0:T(8,128)S(1)}, f32[128,512]{1,0:T(8,128)}, u32[]{:S(2)}) copy-start(f32[128,512]{1,0:T(8,128)} %param.21) | copy-start | bytes 786436
  424.3 370.8 %copy-start.5 = (f32[128,512]{1,0:T(8,128)S(1)}, f32[128,512]{1,0:T(8,128)}, u32[]{:S(2)}) copy-start(f32[128,512]{1,0:T(8,128)} %param.25) | copy-start | bytes 786436
  424.3 370.8 %copy-start.6 = (f32[128,512]{1,0:T(8,128)S(1)}, f32[128,512]{1,0:T(8,128)}, u32[]{:S(2)}) copy-start(f32[128,512]{1,0:T(8,128)} %param.29) | copy-start | bytes 786436
  743.9 51.2 %copy-start.3 = (f32[128,512]{1,0:T(8,128)S(1)}, f32[128,512]{1,0:T(8,128)}, u32[]{:S(2)}) copy-start(f32[128,512]{1,0:T(8,128)} %reduce-scatter.9.cloned.1.call-done) | copy-start | bytes 786436
Sparse Core Ops, SparseCore 0:
  11.4 66.4 all-gather.2
  373.7 17.7 all-reduce.9
  394.4 23.4 all-reduce.11
  420.7 77.2 reduce-scatter.12
  500.6 72.4 reduce-scatter.10
  575.9 74.0 reduce-scatter.6
  652.3 91.5 reduce-scatter.8
where the time goes:
time: 806 us; the launch traced here: 804 us
  waiting for transfers between devices  341 us (42%)
  blocking collectives  323 us (40%)
  other arithmetic  48.4 us (6%)
  matrix products  40.3 us (5%)
  local copies, waits for them, and re-layouts  32.3 us (4%)
  between operations  19 us (2%)
    reduce_scatter x1, waiting for transfers between devices, on_device(): lax.psum_scatter(paired[1], 'dp', scatter_dimension=0, tiled=True)  92.4 us
    reduce_scatter x1, waiting for transfers between devices, on_device(): lax.psum_scatter(paired[0], 'dp', scatter_dimension=2, tiled=True)  75.5 us
    reduce_scatter x1, waiting for transfers between devices, on_device(): lax.psum_scatter(paired[2], 'dp', scatter_dimension=0, tiled=True)  73.8 us
    unnamed x8, waiting for transfers between devices  70 us
    all_gather x1, blocking collectives, on_device(): lax.all_gather(w_class.astype(jnp.bfloat16), 'dp', axis=0, tiled=True)  43.3 us
    all_gather x1, blocking collectives, on_device(): lax.all_gather(small_params.astype(jnp.bfloat16), 'dp', axis=1, tiled=True)  43 us
    psum x1, blocking collectives, on_device(): totals_two = lax.psum((shift2_part, gain2_part), ('dp', 'rep'))  41.4 us
    psum x1, blocking collectives, on_device(): grad_norm = jnp.sqrt(lax.psum(local_squares, 'dp'))  40.5 us
  transfers between devices with their start and end apart: 7, of which 6 were waited for; matrix products, arithmetic and copies ran while one was open for 9% of the time, Pallas kernels for 0%

commit v1 on v0

--- a/solution.py
+++ b/solution.py
@@ -67,8 +67,24 @@
     classes = w_class.shape[1]
     rows = jnp.take(table, batch_index, axis=0)
     input_features = rows.astype(jnp.bfloat16).reshape(batch, HOPS, d_in)
+
+    def expand_the_rings(raw, axis_tag, ndim_at):
+        extent = lax.axis_size(axis_tag)
+        grid = [(k0, (k0 + 1) % extent) for k0 in range(extent)]
+        panels = [(k0, (k0 - 1) % extent) for k0 in range(extent)]
+        v_next, odd = ([raw], [raw])
+        for _ in range(extent // 2):
+            arr_next = lax.ppermute(v_next[-1], axis_tag, grid)
+            v_next.append(arr_next)
+        for _ in range((extent - 1) // 2):
+            b_now = lax.ppermute(odd[-1], axis_tag, panels)
+            odd.append(b_now)
+        a_now = jnp.concatenate([*v_next[::-1], *odd[1:]], ndim_at)
+        a_next = lax.axis_index(axis_tag)
+        return jnp.roll(a_now, (a_next - extent // 2) * raw.shape[ndim_at], ndim_at)
+
     branch_full, merge_full, class_full, small_full = (
-        lax.all_gather(w_branch.astype(jnp.bfloat16), "dp", axis=2, tiled=True),
+        expand_the_rings(w_branch.astype(jnp.bfloat16), "dp", 2),
         lax.all_gather(w_merge.astype(jnp.bfloat16), "dp", axis=0, tiled=True),
         lax.all_gather(w_class.astype(jnp.bfloat16), "dp", axis=0, tiled=True),
         lax.all_gather(small_params.astype(jnp.bfloat16), "dp", axis=1, tiled=True),

time: 806 us -> 823 us (1.021)
  starting transfers between devices: 0.51 us -> 42.5 us
  waiting for transfers between devices: 341 us -> 312 us
    unnamed x8, waiting for transfers between devices: 70 us -> 25.8 us
    ppermute x0 -> x15, starting transfers between devices: none -> 42.3 us  [the longest x7 42.2 us: expand_the_rings(): b_now = lax.ppermute(odd[-1], axis_tag, panels)]
    ppermute x0 -> x15, waiting for transfers between devices: none -> 14.5 us  [the longest x8 11.1 us: expand_the_rings(): arr_next = lax.ppermute(v_next[-1], axis_tag, grid)]
  transfers between devices with their start and end apart: 7 -> 22, of which waited for: 6 -> 15; matrix products, arithmetic and copies ran while one was open for 9% -> 9% of each run, Pallas kernels for 0% -> 0%
where the time goes in v1:
time: 823 us; the launch traced here: 821 us
  blocking collectives  327 us (40%)
  waiting for transfers between devices  312 us (38%)
  other arithmetic  43.6 us (5%)
  starting transfers between devices  42.5 us (5%)
  matrix products  38.5 us (5%)
  local copies, waits for them, and re-layouts  38.3 us (5%)
  between operations  19 us (2%)
    reduce_scatter x1, waiting for transfers between devices, on_device(): lax.psum_scatter(paired[1], 'dp', scatter_dimension=0, tiled=True)  92.5 us
    reduce_scatter x1, waiting for transfers between devices, on_device(): lax.psum_scatter(paired[0], 'dp', scatter_dimension=2, tiled=True)  75.5 us
    reduce_scatter x1, waiting for transfers between devices, on_device(): lax.psum_scatter(paired[2], 'dp', scatter_dimension=0, tiled=True)  73.6 us
    all_gather x1, blocking collectives, on_device(): lax.all_gather(w_branch.astype(jnp.bfloat16), 'dp', axis=2, tiled=True)  44.1 us
    ppermute x7, starting transfers between devices, expand_the_rings(): b_now = lax.ppermute(odd[-1], axis_tag, panels)  42.2 us
    all_gather x1, blocking collectives, on_device(): lax.all_gather(w_class.astype(jnp.bfloat16), 'dp', axis=0, tiled=True)  42 us
    all_gather x1, blocking collectives, on_device(): lax.all_gather(small_params.astype(jnp.bfloat16), 'dp', axis=1, tiled=True)  41.8 us
    psum x1, blocking collectives, on_device(): lax.psum((jnp.sum(pre2, axis=0), jnp.sum(pre2 * pre2, axis=0)), ('dp', 'r...  41 us
  transfers between devices with their start and end apart: 22, of which 15 were waited for; matrix products, arithmetic and copies ran while one was open for 9% of the time, Pallas kernels for 0%

profile of v1, /device:TPU:0, one launch (start us, length us, event | category | flops | bytes accessed | tf_op | source)
XLA Modules:
  0.0 820.9 jit_solution(11482136188271546018)
XLA Ops:
  8.2 7.0 collective-permute-start.8
  15.2 1.6 convert_element_type.82
  17.6 41.8 %all-gather = bf16[16,32,20]{1,2,0:T(8,128)(2,1)S(1)} all-gather(bf16[1,32,20]{1,2,0:T(8,128)(2,1)S(1)} %convert_bitcast_fusion), channel_id=1, replica_groups=mesh['dp'=16,'rep'=2] {'dp'}, dimensions={0}, use_global_device_ids=true | all-gather | bytes 21760 | tf_op jit(solution)/shard_map/all_gather | solution.py:90
  59.6 5.7 collective-permute-start.9
  65.2 2.6 collective-permute-done.1
  67.9 2.1 collective-permute-done.9
  70.0 6.1 collective-permute-start.10
  78.7 6.1 collective-permute-start.11
  84.8 2.2 collective-permute-done.3
  87.1 6.1 collective-permute-start.12
  93.2 2.1 collective-permute-done.4
  96.0 5.7 collective-permute-start.13
  101.6 1.9 collective-permute-done.5
  104.9 5.6 collective-permute-start.14
  113.8 6.9 copy.57
  120.8 6.7 gather_fusion
  128.2 42.0 %all_gather.16 = bf16[512,47]{1,0:T(8,128)(2,1)S(1)} all-gather(bf16[32,47]{1,0:T(8,128)(2,1)} %convert_element_type.84), channel_id=1, replica_groups=mesh['dp'=16,'rep'=2] {'dp'}, dimensions={0}, use_global_device_ids=true | all-gather | bytes 51136 | tf_op jit(solution)/shard_map/all_gather | solution.py:89
  170.2 5.0 concatenate.12
  175.2 4.8 fusion
  180.1 9.2 %copy.61 = f32[1024,2048]{1,0:T(8,128)} copy(f32[1024,2048]{0,1:T(8,128)} %bitcast.69) | data formatting | bytes 16777216 | tf_op jit(solution)/shard_map/reshape | solution.py:103
  189.2 37.2 %all-reduce.4 = (f32[2048]{0:T(1024)S(1)}, f32[2048]{0:T(1024)S(1)}) all-reduce(f32[2048]{0:T(1024)S(1)} %bitcast.95, f32[2048]{0:T(1024)S(1)} %bitcast.94), channel_id=1, replica_groups=mesh['dp'=16,'rep'=2] {'dp','rep'}, use_global_device_ids=true, to_apply=%region_3.4 | all-reduce | flops 4096 | bytes 32768 | tf_op jit(solution)/shard_map/psum | solution.py:104
  226.4 9.1 %add_convert_fusion = bf16[1024,2048]{1,0:T(8,128)(2,1)} fusion(f32[2048]{0:T(1024)S(1)} %get-tuple-element.89, f32[2048]{0:T(1024)S(1)} %bitcast.84, f32[2048]{0:T(1024)S(1)} %broadcast_subtract_fusion.1, f32[2048]{0:T(1024)S(1)} %bitcast.90, f32[2048]{0:T(1024)S(1)} %get-tuple-element.82, f32[1024,2048]{1,0:T(8,128)} %copy.61, ...), kind=kLoop, calls=%fused_computation.10 | loop fusion | flops 39845888 | bytes 12648448 | tf_op jit(solution)/shard_map/convert_element_type | solution.py:112
  235.6 5.2 multiply_reduce_fusion.5
  240.8 41.0 %all-reduce.3 = (f32[512]{0:T(512)S(1)}, f32[512]{0:T(512)S(1)}) all-reduce(f32[512]{0:T(512)S(1)} %get-tuple-element.40, f32[512]{0:T(512)S(1)} %get-tuple-element.39), channel_id=1, replica_groups=mesh['dp'=16,'rep'=2] {'dp','rep'}, use_global_device_ids=true, to_apply=%region_7.8 | all-reduce | flops 1024 | bytes 8192 | tf_op jit(solution)/shard_map/psum | solution.py:114
  284.5 3.0 multiply_reduce_fusion.3
  287.5 40.0 %all-reduce.2 = (f32[512]{0:T(512)S(1)}, f32[512]{0:T(512)S(1)}) all-reduce(f32[512]{0:T(512)S(1)} %get-tuple-element.37, f32[512]{0:T(512)S(1)} %get-tuple-element.38), channel_id=1, replica_groups=mesh['dp'=16,'rep'=2] {'dp','rep'}, use_global_device_ids=true, to_apply=%region_13.14 | all-reduce | flops 1024 | bytes 8192 | tf_op jit(solution)/shard_map/psum | solution.py:135
  327.6 2.4 multiply_convert_fusion.1
  330.4 3.7 convolution_convert_fusion
  334.1 13.9 %multiply_reduce_fusion = (bf16[2048]{0:T(1024)(128)(2,1)S(1)}, bf16[2048]{0:T(1024)(128)(2,1)S(1)}, f32[2048]{0:T(1024)S(1)}, f32[2048]{0:T(1024)S(1)}, f32[1024,2048]{1,0:T(8,128)}) fusion(f32[2048]{0:T(1024)S(1)} %broadcast_subtract_fusion.1, f32[2048]{0:T(1024)S(1)} %bitcast.91, f32[2048]{0:T(1024)S(1)} %get-tuple-element.82, ...), kind=kOutput, calls=%fused_computation.4 | convolution fusion | flops 2225070080 | bytes 20013056 | tf_op jit(solution)/shard_map/dot_general | solution.py:29
  348.1 40.4 %all-reduce.1 = (f32[2048]{0:T(1024)S(1)}, f32[2048]{0:T(1024)S(1)}) all-reduce(f32[2048]{0:T(1024)S(1)} %get-tuple-element.32, f32[2048]{0:T(1024)S(1)} %get-tuple-element.33), channel_id=1, replica_groups=mesh['dp'=16,'rep'=2] {'dp','rep'}, use_global_device_ids=true, to_apply=%region_17.18 | all-reduce | flops 4096 | bytes 32768 | tf_op jit(solution)/shard_map/psum | solution.py:150
  388.6 1.9 concatenate.13
  390.5 7.2 multiply_convert_fusion
  397.8 1.9 copy-done
  399.7 2.5 fusion.10
  402.2 6.7 all-reduce.10.cloned.1.call-done
  409.0 1.6 copy.66
  410.6 1.6 convert_element_type.94
  412.3 23.1 %all-reduce.12.cloned.1.call-done = (bf16[4,100,512]{1,2,0:T(8,128)(2,1)}, bf16[2048,512]{1,0:T(8,128)(2,1)}) async-done(((bf16[4,100,512]{1,2,0:T(8,128)(2,1)}, bf16[2048,512]{1,0:T(8,128)(2,1)}), (bf16[4,100,512]{1,2,0:T(8,128)(2,1)}, bf16[2048,512]{1,0:T(8,128)(2,1)})) %all-reduce.12.cloned.1.call-update) | async-done | bytes 2506768 | tf_op jit(solution)/shard_map/psum | solution.py:181
  435.5 2.1 convert_element_type.90
  437.6 4.2 convert_element_type.92
  441.9 44.1 %all_gather.17 = bf16[4,100,512]{1,0,2:T(4,128)(2,1)S(1)} all-gather(bf16[4,100,32]{1,0,2:T(4,128)(2,1)S(1)} %copy.63), channel_id=1, replica_groups=mesh['dp'=16,'rep'=2] {'dp'}, dimensions={2}, use_global_device_ids=true | all-gather | bytes 435200 | tf_op jit(solution)/shard_map/all_gather | solution.py:125
  486.1 3.7 fusion.7
  489.8 25.7 %reduce-scatter.13.cloned.1.call-done = f32[32,20]{1,0:T(8,128)} async-done(((f32[512,20]{1,0:T(8,128)}), f32[32,20]{1,0:T(8,128)}) %reduce-scatter.13.cloned.1.call-update) | async-done | bytes 2576
  517.0 73.6 %reduce-scatter.11.cloned.1.call-done = f32[32,47]{1,0:T(8,128)} async-done(((f32[512,47]{1,0:T(8,128)}), f32[32,47]{1,0:T(8,128)}) %reduce-scatter.11.cloned.1.call-update) | async-done | bytes 6032 | tf_op jit(solution)/shard_map/reduce_scatter | solution.py:189
  591.9 75.5 %reduce-scatter.7.cloned.1.call-done = f32[4,100,32]{1,2,0:T(8,128)} async-done(((f32[4,100,512]{1,2,0:T(8,128)}), f32[4,100,32]{1,2,0:T(8,128)}) %reduce-scatter.7.cloned.1.call-update) | async-done | bytes 51216 | tf_op jit(solution)/shard_map/reduce_scatter | solution.py:187
  668.9 92.5 %reduce-scatter.9.cloned.1.call-done = f32[128,512]{1,0:T(8,128)} async-done(((f32[2048,512]{1,0:T(8,128)}), f32[128,512]{1,0:T(8,128)}) %reduce-scatter.9.cloned.1.call-update) | async-done | bytes 262160 | tf_op jit(solution)/shard_map/reduce_scatter | solution.py:188
  761.4 1.7 multiply_reduce_fusion.6
  767.0 40.6 %psum.103 = f32[]{:T(128)} all-reduce(f32[]{:T(128)S(6)} %add.247), channel_id=1, replica_groups=mesh['dp'=16,'rep'=2] {'dp'}, use_global_device_ids=true, to_apply=%region_34.35 | all-reduce | flops 1 | bytes 8 | tf_op jit(solution)/shard_map/psum | solution.py:195
  (143 shorter events, 24.5 us)
Async XLA Ops:
  7.2 228.4 %all-gather.3.cloned.1.call-start = ((), (), s32[]{:S(2)}) async-start(), calls=%async_computation.4 | async-start | bytes 2228224 | tf_op jit(solution)/shard_map/all_gather | solution.py:88
  8.2 51.3 %collective-permute-start.8 = (bf16[4,100,32]{2,1,0:T(8,128)(2,1)S(1)}, bf16[4,100,32]{2,1,0:T(8,128)(2,1)S(1)}, u32[]{:S(2)}, u32[]{:S(2)}) collective-permute-start(bf16[4,100,32]{2,1,0:T(8,128)(2,1)S(1)} %copy.59), channel_id=1, source_target_pairs={{0,30},{2,0},{4,2},{6,4},{8,6},{10,8},{12,10},{14,12},{16,14},{18,... | collective-permute-start | bytes 76808 | tf_op jit(solution)/shard_map/ppermute | solution.py:80
  15.2 44.2 %collective-permute-start = (bf16[4,100,32]{2,1,0:T(8,128)(2,1)S(1)}, bf16[4,100,32]{2,1,0:T(8,128)(2,1)S(1)}, u32[]{:S(2)}, u32[]{:S(2)}) collective-permute-start(bf16[4,100,32]{2,1,0:T(8,128)(2,1)S(1)} %copy.59), channel_id=1, source_target_pairs={{0,2},{2,4},{4,6},{6,8},{8,10},{10,12},{12,14},{14,16},{16,18},{18... | collective-permute-start | bytes 76808 | tf_op jit(solution)/shard_map/ppermute | solution.py:77
  16.9 392.1 %all-reduce.10.cloned.1.call-start = ((), (), s32[]{:S(2)}) async-start(), calls=%async_computation.9 | async-start | bytes 311296 | tf_op jit(solution)/shard_map/psum | solution.py:183
  59.4 8.5 %collective-permute-start.1 = (bf16[4,100,32]{2,1,0:T(8,128)(2,1)S(1)}, bf16[4,100,32]{2,1,0:T(8,128)(2,1)S(1)}, u32[]{:S(2)}, u32[]{:S(2)}) collective-permute-start(bf16[4,100,32]{2,1,0:T(8,128)(2,1)S(1)} %collective-permute-done), channel_id=1, source_target_pairs={{0,2},{2,4},{4,6},{6,8},{8,10},{10,12},{12,14},{14,16},{16,18},{18... | collective-permute-start | bytes 76808 | tf_op jit(solution)/shard_map/ppermute | solution.py:77
  59.6 10.4 %collective-permute-start.9 = (bf16[4,100,32]{2,1,0:T(8,128)(2,1)S(1)}, bf16[4,100,32]{2,1,0:T(8,128)(2,1)S(1)}, u32[]{:S(2)}, u32[]{:S(2)}) collective-permute-start(bf16[4,100,32]{2,1,0:T(8,128)(2,1)S(1)} %collective-permute-done.8), channel_id=1, source_target_pairs={{0,30},{2,0},{4,2},{6,4},{8,6},{10,8},{12,10},{14,12},{16,14},{18,... | collective-permute-start | bytes 76808 | tf_op jit(solution)/shard_map/ppermute | solution.py:80
  67.9 9.0 %collective-permute-start.2 = (bf16[4,100,32]{2,1,0:T(8,128)(2,1)S(1)}, bf16[4,100,32]{2,1,0:T(8,128)(2,1)S(1)}, u32[]{:S(2)}, u32[]{:S(2)}) collective-permute-start(bf16[4,100,32]{2,1,0:T(8,128)(2,1)S(1)} %collective-permute-done.1), channel_id=1, source_target_pairs={{0,2},{2,4},{4,6},{6,8},{8,10},{10,12},{12,14},{14,16},{16,18},{18... | collective-permute-start | bytes 76808 | tf_op jit(solution)/shard_map/ppermute | solution.py:77
  70.0 8.7 %collective-permute-start.10 = (bf16[4,100,32]{2,1,0:T(8,128)(2,1)S(1)}, bf16[4,100,32]{2,1,0:T(8,128)(2,1)S(1)}, u32[]{:S(2)}, u32[]{:S(2)}) collective-permute-start(bf16[4,100,32]{2,1,0:T(8,128)(2,1)S(1)} %collective-permute-done.9), channel_id=1, source_target_pairs={{0,30},{2,0},{4,2},{6,4},{8,6},{10,8},{12,10},{14,12},{16,14},{18,... | collective-permute-start | bytes 76808 | tf_op jit(solution)/shard_map/ppermute | solution.py:80
  76.9 10.1 %collective-permute-start.3 = (bf16[4,100,32]{2,1,0:T(8,128)(2,1)S(1)}, bf16[4,100,32]{2,1,0:T(8,128)(2,1)S(1)}, u32[]{:S(2)}, u32[]{:S(2)}) collective-permute-start(bf16[4,100,32]{2,1,0:T(8,128)(2,1)S(1)} %collective-permute-done.2), channel_id=1, source_target_pairs={{0,2},{2,4},{4,6},{6,8},{8,10},{10,12},{12,14},{14,16},{16,18},{18... | collective-permute-start | bytes 76808 | tf_op jit(solution)/shard_map/ppermute | solution.py:77
  78.7 42.0 %copy-start.4 = (bf16[4,100,32]{2,1,0:T(8,128)(2,1)}, bf16[4,100,32]{2,1,0:T(8,128)(2,1)S(1)}, u32[]{:S(2)}) copy-start(bf16[4,100,32]{2,1,0:T(8,128)(2,1)S(1)} %collective-permute-done.10) | copy-start | bytes 76804
  78.7 8.4 %collective-permute-start.11 = (bf16[4,100,32]{2,1,0:T(8,128)(2,1)S(1)}, bf16[4,100,32]{2,1,0:T(8,128)(2,1)S(1)}, u32[]{:S(2)}, u32[]{:S(2)}) collective-permute-start(bf16[4,100,32]{2,1,0:T(8,128)(2,1)S(1)} %collective-permute-done.10), channel_id=1, source_target_pairs={{0,30},{2,0},{4,2},{6,4},{8,6},{10,8},{12,10},{14,12},{16,14},{18,... | collective-permute-start | bytes 76808 | tf_op jit(solution)/shard_map/ppermute | solution.py:80
  87.0 33.8 %copy-start.5 = (bf16[4,100,32]{2,1,0:T(8,128)(2,1)}, bf16[4,100,32]{2,1,0:T(8,128)(2,1)S(1)}, u32[]{:S(2)}) copy-start(bf16[4,100,32]{2,1,0:T(8,128)(2,1)S(1)} %collective-permute-done.3) | copy-start | bytes 76804
  87.0 8.3 %collective-permute-start.4 = (bf16[4,100,32]{2,1,0:T(8,128)(2,1)S(1)}, bf16[4,100,32]{2,1,0:T(8,128)(2,1)S(1)}, u32[]{:S(2)}, u32[]{:S(2)}) collective-permute-start(bf16[4,100,32]{2,1,0:T(8,128)(2,1)S(1)} %collective-permute-done.3), channel_id=1, source_target_pairs={{0,2},{2,4},{4,6},{6,8},{8,10},{10,12},{12,14},{14,16},{16,18},{18... | collective-permute-start | bytes 76808 | tf_op jit(solution)/shard_map/ppermute | solution.py:77
  87.1 33.6 %copy-start.6 = (bf16[4,100,32]{2,1,0:T(8,128)(2,1)}, bf16[4,100,32]{2,1,0:T(8,128)(2,1)S(1)}, u32[]{:S(2)}) copy-start(bf16[4,100,32]{2,1,0:T(8,128)(2,1)S(1)} %collective-permute-done.11) | copy-start | bytes 76804
  87.1 8.9 %collective-permute-start.12 = (bf16[4,100,32]{2,1,0:T(8,128)(2,1)S(1)}, bf16[4,100,32]{2,1,0:T(8,128)(2,1)S(1)}, u32[]{:S(2)}, u32[]{:S(2)}) collective-permute-start(bf16[4,100,32]{2,1,0:T(8,128)(2,1)S(1)} %collective-permute-done.11), channel_id=1, source_target_pairs={{0,30},{2,0},{4,2},{6,4},{8,6},{10,8},{12,10},{14,12},{16,14},{18,... | collective-permute-start | bytes 76808 | tf_op jit(solution)/shard_map/ppermute | solution.py:80
  95.3 25.5 %copy-start.7 = (bf16[4,100,32]{2,1,0:T(8,128)(2,1)}, bf16[4,100,32]{2,1,0:T(8,128)(2,1)S(1)}, u32[]{:S(2)}) copy-start(bf16[4,100,32]{2,1,0:T(8,128)(2,1)S(1)} %collective-permute-done.4) | copy-start | bytes 76804
  95.3 8.3 %collective-permute-start.5 = (bf16[4,100,32]{2,1,0:T(8,128)(2,1)S(1)}, bf16[4,100,32]{2,1,0:T(8,128)(2,1)S(1)}, u32[]{:S(2)}, u32[]{:S(2)}) collective-permute-start(bf16[4,100,32]{2,1,0:T(8,128)(2,1)S(1)} %collective-permute-done.4), channel_id=1, source_target_pairs={{0,2},{2,4},{4,6},{6,8},{8,10},{10,12},{12,14},{14,16},{16,18},{18... | collective-permute-start | bytes 76808 | tf_op jit(solution)/shard_map/ppermute | solution.py:77
  96.0 24.8 %copy-start.8 = (bf16[4,100,32]{2,1,0:T(8,128)(2,1)}, bf16[4,100,32]{2,1,0:T(8,128)(2,1)S(1)}, u32[]{:S(2)}) copy-start(bf16[4,100,32]{2,1,0:T(8,128)(2,1)S(1)} %collective-permute-done.12) | copy-start | bytes 76804
  96.0 8.9 %collective-permute-start.13 = (bf16[4,100,32]{2,1,0:T(8,128)(2,1)S(1)}, bf16[4,100,32]{2,1,0:T(8,128)(2,1)}, u32[]{:S(2)}, u32[]{:S(2)}) collective-permute-start(bf16[4,100,32]{2,1,0:T(8,128)(2,1)S(1)} %collective-permute-done.12), channel_id=1, source_target_pairs={{0,30},{2,0},{4,2},{6,4},{8,6},{10,8},{12,10},{14,12},{16,14},{18,... | collective-permute-start | bytes 76808 | tf_op jit(solution)/shard_map/ppermute | solution.py:80
  103.6 17.2 %copy-start.9 = (bf16[4,100,32]{2,1,0:T(8,128)(2,1)}, bf16[4,100,32]{2,1,0:T(8,128)(2,1)S(1)}, u32[]{:S(2)}) copy-start(bf16[4,100,32]{2,1,0:T(8,128)(2,1)S(1)} %collective-permute-done.5) | copy-start | bytes 76804
  103.6 8.4 %collective-permute-start.6 = (bf16[4,100,32]{2,1,0:T(8,128)(2,1)S(1)}, bf16[4,100,32]{2,1,0:T(8,128)(2,1)}, u32[]{:S(2)}, u32[]{:S(2)}) collective-permute-start(bf16[4,100,32]{2,1,0:T(8,128)(2,1)S(1)} %collective-permute-done.5), channel_id=1, source_target_pairs={{0,2},{2,4},{4,6},{6,8},{8,10},{10,12},{12,14},{14,16},{16,18},{18... | collective-permute-start | bytes 76808 | tf_op jit(solution)/shard_map/ppermute | solution.py:77
  104.9 65.3 %collective-permute-start.14 = (bf16[4,100,32]{2,1,0:T(8,128)(2,1)}, bf16[4,100,32]{2,1,0:T(8,128)(2,1)}, u32[]{:S(2)}, u32[]{:S(2)}) collective-permute-start(bf16[4,100,32]{2,1,0:T(8,128)(2,1)} %collective-permute-done.13), channel_id=1, source_target_pairs={{0,30},{2,0},{4,2},{6,4},{8,6},{10,8},{12,10},{14,12},{16,14},{18,... | collective-permute-start | bytes 76808 | tf_op jit(solution)/shard_map/ppermute | solution.py:80
  112.0 58.2 %collective-permute-start.7 = (bf16[4,100,32]{2,1,0:T(8,128)(2,1)}, bf16[4,100,32]{2,1,0:T(8,128)(2,1)}, u32[]{:S(2)}, u32[]{:S(2)}) collective-permute-start(bf16[4,100,32]{2,1,0:T(8,128)(2,1)} %collective-permute-done.6), channel_id=1, source_target_pairs={{0,2},{2,4},{4,6},{6,8},{8,10},{10,12},{12,14},{14,16},{16,18},{18... | collective-permute-start | bytes 76808 | tf_op jit(solution)/shard_map/ppermute | solution.py:77
  127.5 47.7 %copy-start.24 = (pred[1024]{0:T(1024)(128)(4,1)S(1)}, pred[1024]{0:T(1024)(128)(4,1)}, u32[]{:S(2)}) copy-start(pred[1024]{0:T(1024)(128)(4,1)} %compare_and_fusion) | copy-start | bytes 3076
  235.5 46.3 %copy-start.21 = (f32[1,512]{1,0:T(1,128)S(1)}, f32[1,512]{1,0:T(1,128)}, u32[]{:S(2)}) copy-start(f32[1,512]{1,0:T(1,128)} %get-tuple-element.75) | copy-start | bytes 6148
  235.5 46.3 %copy-start.22 = (f32[1,512]{1,0:T(1,128)S(1)}, f32[1,512]{1,0:T(1,128)}, u32[]{:S(2)}) copy-start(f32[1,512]{1,0:T(1,128)} %get-tuple-element.76) | copy-start | bytes 6148
  235.5 47.2 %copy-start.26 = (f32[47]{0:T(128)S(1)}, f32[47]{0:T(128)}, u32[]{:S(2)}) copy-start(f32[47]{0:T(128)} %slice_bitcast_fusion.4) | copy-start | bytes 568
  240.8 42.4 %copy-start.23 = (s32[1024]{0:T(1024)S(1)}, s32[1024]{0:T(1024)}, u32[]{:S(2)}) copy-start(s32[1024]{0:T(1024)} %param.19) | copy-start | bytes 12292
  327.6 6.6 slice-start
  390.5 45.0 %all-reduce.12.cloned.1.call-start = ((), (), s32[]{:S(2)}) async-start(), calls=%async_computation.10 | async-start | bytes 5242880 | tf_op jit(solution)/shard_map/psum | solution.py:181
  390.5 9.2 %copy-start.25 = (pred[1024]{0:T(1024)(128)(4,1)S(1)}, pred[1024]{0:T(1024)(128)(4,1)}, u32[]{:S(2)}) copy-start(pred[1024]{0:T(1024)(128)(4,1)} %compare_and_fusion) | copy-start | bytes 3076
  402.2 113.4 %reduce-scatter.13.cloned.1.call-start = ((), (), s32[]{:S(2)}) async-start(), calls=%async_computation.8 | async-start | bytes 278528
  410.6 180.0 %reduce-scatter.11.cloned.1.call-start = ((), (), s32[]{:S(2)}) async-start(), calls=%async_computation.7 | async-start | bytes 278528 | tf_op jit(solution)/shard_map/reduce_scatter | solution.py:189
  412.3 255.1 %reduce-scatter.7.cloned.1.call-start = ((), (), s32[]{:S(2)}) async-start(), calls=%async_computation.5 | async-start | bytes 1114112 | tf_op jit(solution)/shard_map/reduce_scatter | solution.py:187
  437.6 323.8 %reduce-scatter.9.cloned.1.call-start = ((), (), s32[]{:S(2)}) async-start(), calls=%async_computation.6 | async-start | bytes 4456448 | tf_op jit(solution)/shard_map/reduce_scatter | solution.py:188
  486.0 322.3 %copy-start.16 = (f32[20,32]{1,0:T(8,128)S(1)}, f32[20,32]{1,0:T(8,128)}, u32[]{:S(2)}) copy-start(f32[20,32]{1,0:T(8,128)} %param.23) | copy-start | bytes 7684
  486.0 322.3 %copy-start.19 = (f32[20,32]{1,0:T(8,128)S(1)}, f32[20,32]{1,0:T(8,128)}, u32[]{:S(2)}) copy-start(f32[20,32]{1,0:T(8,128)} %param.27) | copy-start | bytes 7684
  486.0 322.3 %copy-start.20 = (f32[20,32]{1,0:T(8,128)S(1)}, f32[20,32]{1,0:T(8,128)}, u32[]{:S(2)}) copy-start(f32[20,32]{1,0:T(8,128)} %param.31) | copy-start | bytes 7684
  486.0 323.0 %copy-start.15 = (f32[32,47]{1,0:T(8,128)S(1)}, f32[32,47]{1,0:T(8,128)}, u32[]{:S(2)}) copy-start(f32[32,47]{1,0:T(8,128)} %param.22) | copy-start | bytes 18052
  486.0 323.0 %copy-start.17 = (f32[32,47]{1,0:T(8,128)S(1)}, f32[32,47]{1,0:T(8,128)}, u32[]{:S(2)}) copy-start(f32[32,47]{1,0:T(8,128)} %param.26) | copy-start | bytes 18052
  486.0 323.0 %copy-start.18 = (f32[32,47]{1,0:T(8,128)S(1)}, f32[32,47]{1,0:T(8,128)}, u32[]{:S(2)}) copy-start(f32[32,47]{1,0:T(8,128)} %param.30) | copy-start | bytes 18052
  486.0 324.3 %copy-start.12 = (f32[4,100,32]{1,2,0:T(8,128)S(1)}, f32[4,100,32]{1,2,0:T(8,128)}, u32[]{:S(2)}) copy-start(f32[4,100,32]{1,2,0:T(8,128)} %param.20) | copy-start | bytes 153604
  486.0 324.3 %copy-start.13 = (f32[4,100,32]{1,2,0:T(8,128)S(1)}, f32[4,100,32]{1,2,0:T(8,128)}, u32[]{:S(2)}) copy-start(f32[4,100,32]{1,2,0:T(8,128)} %param.24) | copy-start | bytes 153604
  486.0 324.3 %copy-start.14 = (f32[4,100,32]{1,2,0:T(8,128)S(1)}, f32[4,100,32]{1,2,0:T(8,128)}, u32[]{:S(2)}) copy-start(f32[4,100,32]{1,2,0:T(8,128)} %param.28) | copy-start | bytes 153604
  486.0 325.8 %copy-start.2 = (f32[128,512]{1,0:T(8,128)S(1)}, f32[128,512]{1,0:T(8,128)}, u32[]{:S(2)}) copy-start(f32[128,512]{1,0:T(8,128)} %param.21) | copy-start | bytes 786436
  486.1 325.8 %copy-start.10 = (f32[128,512]{1,0:T(8,128)S(1)}, f32[128,512]{1,0:T(8,128)}, u32[]{:S(2)}) copy-start(f32[128,512]{1,0:T(8,128)} %param.25) | copy-start | bytes 786436
  486.1 325.8 %copy-start.11 = (f32[128,512]{1,0:T(8,128)S(1)}, f32[128,512]{1,0:T(8,128)}, u32[]{:S(2)}) copy-start(f32[128,512]{1,0:T(8,128)} %param.29) | copy-start | bytes 786436
  761.4 50.5 %copy-start.3 = (f32[128,512]{1,0:T(8,128)S(1)}, f32[128,512]{1,0:T(8,128)}, u32[]{:S(2)}) copy-start(f32[128,512]{1,0:T(8,128)} %reduce-scatter.9.cloned.1.call-done) | copy-start | bytes 786436
  (4 other events, 12.3 us)
Sparse Core Ops, SparseCore 0:
  17.0 70.6 all-gather.2
  390.6 18.3 all-reduce.9
  412.0 23.4 all-reduce.11
  438.2 77.2 reduce-scatter.12
  518.2 72.3 reduce-scatter.10
  593.4 74.0 reduce-scatter.6
  669.7 91.6 reduce-scatter.8
